TPU v7x, 512 devices: a whole 4x4x16 slice. The times are simulated.
512 devices in a mesh: row: 16 (over z), col: 16 (over x, y), layer: 2 (over core).
Axes of the slice: x: 4, y: 4, z: 16, core: 2. Of those that a mesh axis runs over, the one named last changes fastest.
Arguments:
- a_tiles: bfloat16 [16, 16, 2, 512, 512], P('row', 'col'), as said below
- a_where: int32 [16, 16, 2], P('row', 'col'), may hold values from 0 to 3, as said below
- a_count: int32 [16, 16], P('row', 'col'), may hold values from 1 to 2, as said below
- b_slab: bfloat16 [16, 16, 1024, 384], P('row', 'col'), may hold values from -6 to 6
Outputs:
- flow_next: float32 [16384, 6144], P(('row', 'layer'), 'col')
Inputs may be any that keep to these rules, and one draw needn't show every extreme that they name: `a_where`: the positions of the slots of one block are distinct. The live slots of a block are its first a_count ones; some block has all 2 slots live. `a_tiles`: entries of slots that are not live are ignored.
All inputs are finite; a program needn't handle non-finite values.
Results may differ from a plain program's by a relative error of at most 0.0003.
Values may be sent and summed in bfloat16 or wider, within the bound.
No kernel may reach another device: no remote copies, remote signals or barrier semaphores. Data moves between devices by JAX's collectives and lax.ppermute only.
A program may use at most 64 MiB of HBM per device.

v0:
```python
import jax
import jax.numpy as jnp
from jax import lax
from jax.sharding import PartitionSpec as P

SPAN = 2


def from_behind(value, axis, steps):
    count = lax.axis_size(axis)
    pairs = [(source, (source + steps) % count) for source in range(count)]
    return lax.ppermute(value, axis, pairs)


def tile_products(partial_sum, tile_data, tile_place, live_count, slab_block):
    tile_size = tile_data.shape[-1]
    slab_cols = slab_block.shape[-1]
    slab_rows = slab_block.reshape(SPAN, tile_size, slab_cols)
    tile_rows = jnp.arange(SPAN, dtype=jnp.int32)
    for slot_index in range(tile_data.shape[0]):
        position = tile_place[slot_index]
        source = lax.dynamic_index_in_dim(slab_rows, position % SPAN, 0, keepdims=False)
        product = jnp.dot(tile_data[slot_index], source, preferred_element_type=jnp.float32)
        live_mask = (slot_index < live_count).astype(jnp.float32)
        target = (tile_rows == position // SPAN).astype(jnp.float32) * live_mask
        partial_sum = partial_sum + target[:, None, None] * product[None]
    return partial_sum


def local(a_tiles, a_where, a_count, b_slab):
    tile_data = a_tiles[0, 0]
    tile_place = a_where[0, 0]
    live_count = a_count[0, 0]
    slab_block = b_slab[0, 0]
    layer_index = lax.axis_index("layer")
    grid_size = lax.axis_size("col")
    rounds = grid_size // lax.axis_size("layer")
    tile_size = tile_data.shape[-1]
    slab_cols = slab_block.shape[-1]
    partial_sum = jnp.zeros((SPAN, tile_size, slab_cols), jnp.float32)
    moved_tiles = from_behind((tile_data, tile_place, live_count), "col", -rounds)
    moved_slab = from_behind(slab_block, "row", -rounds)
    upper = layer_index == 1
    tile_data = jnp.where(upper, moved_tiles[0], tile_data)
    tile_place = jnp.where(upper, moved_tiles[1], tile_place)
    live_count = jnp.where(upper, moved_tiles[2], live_count)
    slab_block = jnp.where(upper, moved_slab, slab_block)
    for turn_index in range(rounds):
        partial_sum = tile_products(partial_sum, tile_data, tile_place, live_count, slab_block)
        if turn_index + 1 < rounds:
            tile_data, tile_place, live_count = from_behind(
                (tile_data, tile_place, live_count), "col", -1
            )
            slab_block = from_behind(slab_block, "row", -1)
    partial_block = partial_sum.reshape(SPAN * tile_size, slab_cols)
    matrix_order = grid_size * SPAN * tile_size
    shared = lax.psum_scatter(partial_block, "layer", scatter_dimension=0, tiled=True)
    inflated = shared * shared
    column_mass = lax.psum(jnp.sum(inflated, axis=0), ("row", "layer"))
    return inflated / (column_mass / matrix_order + 1e-06)


def solution(mesh):
    in_specs = (
        P("row", "col", None, None, None),
        P("row", "col", None),
        P("row", "col"),
        P("row", "col", None, None),
    )
    out_specs = P(("row", "layer"), "col")
    return jax.shard_map(local, mesh=mesh, in_specs=in_specs, out_specs=out_specs, check_vma=False)
```

profile of v0, /device:TPU:2, one launch (start us, length us, event | category | flops | bytes accessed | tf_op | source)
XLA Modules:
  0.0 409.8 jit_solution(3143512087581438021)
XLA Ops:
  13.9 15.7 %collective-permute-start.3 = (bf16[1024,384]{1,0:T(8,128)(2,1)}, bf16[1024,384]{1,0:T(8,128)(2,1)}, u32[]{:S(2)}, u32[]{:S(2)}) collective-permute-start(bf16[1024,384]{1,0:T(8,128)(2,1)} %bitcast.271), channel_id=1, source_target_pairs={{0,256},{32,288},{64,320},{96,352},{128,384},{160,416},{192,448},{... | collective-permute-start | bytes 2359304 | tf_op jit(solution)/shard_map/ppermute | solution.py:12
  29.6 4.0 collective-permute-start.2
  34.9 20.6 %collective-permute-start.5 = (s32[]{:T(128)}, s32[]{:T(128)}, u32[]{:S(2)}, u32[]{:S(2)}) collective-permute-start(s32[]{:T(128)} %select_n.195), channel_id=1, source_target_pairs={{0,30},{2,0},{4,2},{6,4},{8,6},{10,8},{12,10},{14,12},{16,14},{18,... | collective-permute-start | bytes 20 | tf_op jit(solution)/shard_map/ppermute | solution.py:12
  71.9 4.0 collective-permute-start.13
  92.0 4.0 collective-permute-start.21
  110.4 4.3 %collective-permute-start.25 = (s32[]{:T(128)}, s32[]{:T(128)}, u32[]{:S(2)}, u32[]{:S(2)}) collective-permute-start(s32[]{:T(128)} %collective-permute-done.21), channel_id=1, source_target_pairs={{0,30},{2,0},{4,2},{6,4},{8,6},{10,8},{12,10},{14,12},{16,14},{18,... | collective-permute-start | bytes 20 | tf_op jit(solution)/shard_map/ppermute | solution.py:12
  114.7 11.8 %collective-permute-done.25 = s32[]{:T(128)} collective-permute-done((s32[]{:T(128)}, s32[]{:T(128)}, u32[]{:S(2)}, u32[]{:S(2)}) %collective-permute-start.25) | collective-permute-done | bytes 36 | tf_op jit(solution)/shard_map/ppermute | solution.py:12
  127.5 4.3 %collective-permute-start.29 = (s32[]{:T(128)}, s32[]{:T(128)}, u32[]{:S(2)}, u32[]{:S(2)}) collective-permute-start(s32[]{:T(128)} %collective-permute-done.25), channel_id=1, source_target_pairs={{0,30},{2,0},{4,2},{6,4},{8,6},{10,8},{12,10},{14,12},{16,14},{18,... | collective-permute-start | bytes 20 | tf_op jit(solution)/shard_map/ppermute | solution.py:12
  141.0 5.6 %collective-permute-start.16 = (s32[2]{0:T(128)S(1)}, s32[2]{0:T(128)S(1)}, u32[]{:S(2)}, u32[]{:S(2)}) collective-permute-start(s32[2]{0:T(128)S(1)} %collective-permute-done.12), channel_id=1, source_target_pairs={{0,30},{2,0},{4,2},{6,4},{8,6},{10,8},{12,10},{14,12},{16,14},{18,... | collective-permute-start | bytes 32 | tf_op jit(solution)/shard_map/ppermute | solution.py:12
  146.6 12.9 %collective-permute-done.16 = s32[2]{0:T(128)S(1)} collective-permute-done((s32[2]{0:T(128)S(1)}, s32[2]{0:T(128)S(1)}, u32[]{:S(2)}, u32[]{:S(2)}) %collective-permute-start.16) | collective-permute-done | bytes 40 | tf_op jit(solution)/shard_map/ppermute | solution.py:12
  170.1 4.3 %collective-permute-start.14 = (bf16[2,512,512]{2,1,0:T(8,128)(2,1)}, bf16[2,512,512]{2,1,0:T(8,128)(2,1)}, u32[]{:S(2)}, u32[]{:S(2)}) collective-permute-start(bf16[2,512,512]{2,1,0:T(8,128)(2,1)} %collective-permute-done.10), channel_id=1, source_target_pairs={{0,30},{2,0},{4,2},{6,4},{8,6},{10,8},{12,10},{14,12},{16,14},{18,... | collective-permute-start | bytes 3145736 | tf_op jit(solution)/shard_map/ppermute | solution.py:12
  176.5 15.9 %collective-permute-done.20 = s32[2]{0:T(128)S(1)} collective-permute-done((s32[2]{0:T(128)S(1)}, s32[2]{0:T(128)S(1)}, u32[]{:S(2)}, u32[]{:S(2)}) %collective-permute-start.20) | collective-permute-done | bytes 40 | tf_op jit(solution)/shard_map/ppermute | solution.py:12
  200.7 6.5 %collective-permute-start.24 = (s32[2]{0:T(128)S(1)}, s32[2]{0:T(128)S(1)}, u32[]{:S(2)}, u32[]{:S(2)}) collective-permute-start(s32[2]{0:T(128)S(1)} %collective-permute-done.20), channel_id=1, source_target_pairs={{0,30},{2,0},{4,2},{6,4},{8,6},{10,8},{12,10},{14,12},{16,14},{18,... | collective-permute-start | bytes 32 | tf_op jit(solution)/shard_map/ppermute | solution.py:12
  214.5 6.3 %collective-permute-start.18 = (bf16[2,512,512]{2,1,0:T(8,128)(2,1)}, bf16[2,512,512]{2,1,0:T(8,128)(2,1)}, u32[]{:S(2)}, u32[]{:S(2)}) collective-permute-start(bf16[2,512,512]{2,1,0:T(8,128)(2,1)} %collective-permute-done.14), channel_id=1, source_target_pairs={{0,30},{2,0},{4,2},{6,4},{8,6},{10,8},{12,10},{14,12},{16,14},{18,... | collective-permute-start | bytes 3145736 | tf_op jit(solution)/shard_map/ppermute | solution.py:12
  224.9 11.7 %collective-permute-done.28 = s32[2]{0:T(128)S(1)} collective-permute-done((s32[2]{0:T(128)S(1)}, s32[2]{0:T(128)S(1)}, u32[]{:S(2)}, u32[]{:S(2)}) %collective-permute-start.28) | collective-permute-done | bytes 40 | tf_op jit(solution)/shard_map/ppermute | solution.py:12
  244.7 6.5 %collective-permute-start.22 = (bf16[2,512,512]{2,1,0:T(8,128)(2,1)}, bf16[2,512,512]{2,1,0:T(8,128)(2,1)}, u32[]{:S(2)}, u32[]{:S(2)}) collective-permute-start(bf16[2,512,512]{2,1,0:T(8,128)(2,1)} %collective-permute-done.18), channel_id=1, source_target_pairs={{0,30},{2,0},{4,2},{6,4},{8,6},{10,8},{12,10},{14,12},{16,14},{18,... | collective-permute-start | bytes 3145736 | tf_op jit(solution)/shard_map/ppermute | solution.py:12
  252.2 8.7 %collective-permute-done.19 = bf16[1024,384]{1,0:T(8,128)(2,1)} collective-permute-done((bf16[1024,384]{1,0:T(8,128)(2,1)}, bf16[1024,384]{1,0:T(8,128)(2,1)}, u32[]{:S(2)}, u32[]{:S(2)}) %collective-permute-start.19) | collective-permute-done | bytes 786464 | tf_op jit(solution)/shard_map/ppermute | solution.py:12
  268.0 6.5 %collective-permute-start.26 = (bf16[2,512,512]{2,1,0:T(8,128)(2,1)}, bf16[2,512,512]{2,1,0:T(8,128)(2,1)S(1)}, u32[]{:S(2)}, u32[]{:S(2)}) collective-permute-start(bf16[2,512,512]{2,1,0:T(8,128)(2,1)} %collective-permute-done.22), channel_id=1, source_target_pairs={{0,30},{2,0},{4,2},{6,4},{8,6},{10,8},{12,10},{14,12},{16,14},{18,... | collective-permute-start | bytes 3145736 | tf_op jit(solution)/shard_map/ppermute | solution.py:12
  287.4 4.3 %collective-permute-done.26 = bf16[2,512,512]{2,1,0:T(8,128)(2,1)S(1)} collective-permute-done((bf16[2,512,512]{2,1,0:T(8,128)(2,1)}, bf16[2,512,512]{2,1,0:T(8,128)(2,1)S(1)}, u32[]{:S(2)}, u32[]{:S(2)}) %collective-permute-start.26) | collective-permute-done | bytes 1048608 | tf_op jit(solution)/shard_map/ppermute | solution.py:12
  291.7 6.4 %collective-permute-start.30 = (bf16[2,512,512]{2,1,0:T(8,128)(2,1)S(1)}, bf16[2,512,512]{2,1,0:T(8,128)(2,1)S(1)}, u32[]{:S(2)}, u32[]{:S(2)}) collective-permute-start(bf16[2,512,512]{2,1,0:T(8,128)(2,1)S(1)} %collective-permute-done.26), channel_id=1, source_target_pairs={{0,30},{2,0},{4,2},{6,4},{8,6},{10,8},{12,10},{14,12},{16,14},{18,... | collective-permute-start | bytes 3145736 | tf_op jit(solution)/shard_map/ppermute | solution.py:12
  310.0 4.5 %collective-permute-done.31 = bf16[1024,384]{1,0:T(8,128)(2,1)S(1)} collective-permute-done((bf16[1024,384]{1,0:T(8,128)(2,1)S(1)}, bf16[1024,384]{1,0:T(8,128)(2,1)S(1)}, u32[]{:S(2)}, u32[]{:S(2)}) %collective-permute-start.31) | collective-permute-done | bytes 786464 | tf_op jit(solution)/shard_map/ppermute | solution.py:12
  317.1 6.3 %fusion = f32[1024,384]{1,0:T(8,128)} fusion(f32[512,384]{1,0:T(8,128)} %fusion.15, f32[1024]{0:T(1024)S(1)} %bitcast.292, f32[512,384]{1,0:T(8,128)} %fusion.16, f32[1024]{0:T(1024)S(1)} %bitcast.293, f32[512,384]{1,0:T(8,128)} %fusion.17, f32[1024]{0:T(1024)S(1)} %bitcast.290, f32[512,384]{1,0:T(8,128)} %fusion.18, f32[1024]{0:T(1024)S(1)} %bitcast.291, ...), kind=kLoop, calls=%fused_computation.1 | loop fusion | flops 12189696 | bytes 14221312 | tf_op jit(solution)/shard_map/add | solution.py:26
  323.4 26.6 %reduce-scatter.2.cloned.1.call-done = f32[512,384]{1,0:T(8,128)} async-done(((f32[1024,384]{1,0:T(8,128)}), f32[512,384]{1,0:T(8,128)}) %reduce-scatter.2.cloned.1.call-update) | async-done | bytes 786448 | tf_op jit(solution)/shard_map/reduce_scatter | solution.py:57
  351.3 49.6 %psum.7 = f32[384]{0:T(512)S(1)} all-reduce(f32[384]{0:T(512)S(1)} %multiply_reduce_fusion), channel_id=1, replica_groups=mesh['row'=16,'col'=16,'layer'=2] {'row','layer'}, use_global_device_ids=true, to_apply=%region_2.3 | all-reduce | flops 384 | bytes 3072 | tf_op jit(solution)/shard_map/psum | solution.py:59
  (123 shorter events, 93.5 us)
Async XLA Ops:
  6.5 343.5 %reduce-scatter.2.cloned.1.call-start = ((), (), s32[]{:S(2)}) async-start(), calls=%async_computation.1 | async-start | bytes 2359296 | tf_op jit(solution)/shard_map/reduce_scatter | solution.py:57
  6.5 49.0 %collective-permute-start = (s32[2]{0:T(128)}, s32[2]{0:T(128)S(1)}, u32[]{:S(2)}, u32[]{:S(2)}) collective-permute-start(s32[2]{0:T(128)} %bitcast.294), channel_id=1, source_target_pairs={{0,16},{2,18},{4,20},{6,22},{8,24},{10,26},{12,28},{14,30},{16,0},... | collective-permute-start | bytes 32 | tf_op jit(solution)/shard_map/ppermute | solution.py:12
  10.6 23.7 %collective-permute-start.1 = (s32[]{:T(128)}, s32[]{:T(128)}, u32[]{:S(2)}, u32[]{:S(2)}) collective-permute-start(s32[]{:T(128)} %bitcast.2), channel_id=1, source_target_pairs={{0,16},{2,18},{4,20},{6,22},{8,24},{10,26},{12,28},{14,30},{16,0},... | collective-permute-start | bytes 20 | tf_op jit(solution)/shard_map/ppermute | solution.py:12
  13.9 151.1 %collective-permute-start.3 = (bf16[1024,384]{1,0:T(8,128)(2,1)}, bf16[1024,384]{1,0:T(8,128)(2,1)}, u32[]{:S(2)}, u32[]{:S(2)}) collective-permute-start(bf16[1024,384]{1,0:T(8,128)(2,1)} %bitcast.271), channel_id=1, source_target_pairs={{0,256},{32,288},{64,320},{96,352},{128,384},{160,416},{192,448},{... | collective-permute-start | bytes 2359304 | tf_op jit(solution)/shard_map/ppermute | solution.py:12
  29.6 72.4 %collective-permute-start.2 = (bf16[2,512,512]{2,1,0:T(8,128)(2,1)}, bf16[2,512,512]{2,1,0:T(8,128)(2,1)S(1)}, u32[]{:S(2)}, u32[]{:S(2)}) collective-permute-start(bf16[2,512,512]{2,1,0:T(8,128)(2,1)} %bitcast.270), channel_id=1, source_target_pairs={{0,16},{2,18},{4,20},{6,22},{8,24},{10,26},{12,28},{14,30},{16,0},... | collective-permute-start | bytes 3145736 | tf_op jit(solution)/shard_map/ppermute | solution.py:12
  34.9 29.0 %collective-permute-start.5 = (s32[]{:T(128)}, s32[]{:T(128)}, u32[]{:S(2)}, u32[]{:S(2)}) collective-permute-start(s32[]{:T(128)} %select_n.195), channel_id=1, source_target_pairs={{0,30},{2,0},{4,2},{6,4},{8,6},{10,8},{12,10},{14,12},{16,14},{18,... | collective-permute-start | bytes 20 | tf_op jit(solution)/shard_map/ppermute | solution.py:12
  92.0 17.1 %collective-permute-start.21 = (s32[]{:T(128)}, s32[]{:T(128)}, u32[]{:S(2)}, u32[]{:S(2)}) collective-permute-start(s32[]{:T(128)} %collective-permute-done.17), channel_id=1, source_target_pairs={{0,30},{2,0},{4,2},{6,4},{8,6},{10,8},{12,10},{14,12},{16,14},{18,... | collective-permute-start | bytes 20 | tf_op jit(solution)/shard_map/ppermute | solution.py:12
  103.4 34.2 %collective-permute-start.6 = (bf16[2,512,512]{2,1,0:T(8,128)(2,1)S(1)}, bf16[2,512,512]{2,1,0:T(8,128)(2,1)S(1)}, u32[]{:S(2)}, u32[]{:S(2)}) collective-permute-start(bf16[2,512,512]{2,1,0:T(8,128)(2,1)S(1)} %broadcast_select_fusion), channel_id=1, source_target_pairs={{0,30},{2,0},{4,2},{6,4},{8,6},{10,8},{12,10},{14,12},{16,14},{18,... | collective-permute-start | bytes 3145736 | tf_op jit(solution)/shard_map/ppermute | solution.py:12
  105.5 26.4 %collective-permute-start.12 = (s32[2]{0:T(128)S(1)}, s32[2]{0:T(128)S(1)}, u32[]{:S(2)}, u32[]{:S(2)}) collective-permute-start(s32[2]{0:T(128)S(1)} %collective-permute-done.8), channel_id=1, source_target_pairs={{0,30},{2,0},{4,2},{6,4},{8,6},{10,8},{12,10},{14,12},{16,14},{18,... | collective-permute-start | bytes 32 | tf_op jit(solution)/shard_map/ppermute | solution.py:12
  110.4 16.1 %collective-permute-start.25 = (s32[]{:T(128)}, s32[]{:T(128)}, u32[]{:S(2)}, u32[]{:S(2)}) collective-permute-start(s32[]{:T(128)} %collective-permute-done.21), channel_id=1, source_target_pairs={{0,30},{2,0},{4,2},{6,4},{8,6},{10,8},{12,10},{14,12},{16,14},{18,... | collective-permute-start | bytes 20 | tf_op jit(solution)/shard_map/ppermute | solution.py:12
  137.6 32.4 %collective-permute-start.10 = (bf16[2,512,512]{2,1,0:T(8,128)(2,1)S(1)}, bf16[2,512,512]{2,1,0:T(8,128)(2,1)}, u32[]{:S(2)}, u32[]{:S(2)}) collective-permute-start(bf16[2,512,512]{2,1,0:T(8,128)(2,1)S(1)} %collective-permute-done.6), channel_id=1, source_target_pairs={{0,30},{2,0},{4,2},{6,4},{8,6},{10,8},{12,10},{14,12},{16,14},{18,... | collective-permute-start | bytes 3145736 | tf_op jit(solution)/shard_map/ppermute | solution.py:12
  141.0 18.5 %collective-permute-start.16 = (s32[2]{0:T(128)S(1)}, s32[2]{0:T(128)S(1)}, u32[]{:S(2)}, u32[]{:S(2)}) collective-permute-start(s32[2]{0:T(128)S(1)} %collective-permute-done.12), channel_id=1, source_target_pairs={{0,30},{2,0},{4,2},{6,4},{8,6},{10,8},{12,10},{14,12},{16,14},{18,... | collective-permute-start | bytes 32 | tf_op jit(solution)/shard_map/ppermute | solution.py:12
  166.3 32.2 %collective-permute-start.7 = (bf16[1024,384]{1,0:T(8,128)(2,1)S(1)}, bf16[1024,384]{1,0:T(8,128)(2,1)}, u32[]{:S(2)}, u32[]{:S(2)}) collective-permute-start(bf16[1024,384]{1,0:T(8,128)(2,1)S(1)} %broadcast_select_fusion.1), channel_id=1, source_target_pairs={{0,480},{32,0},{64,32},{96,64},{128,96},{160,128},{192,160},{224,1... | collective-permute-start | bytes 2359304 | tf_op jit(solution)/shard_map/ppermute | solution.py:12
  170.1 44.3 %collective-permute-start.14 = (bf16[2,512,512]{2,1,0:T(8,128)(2,1)}, bf16[2,512,512]{2,1,0:T(8,128)(2,1)}, u32[]{:S(2)}, u32[]{:S(2)}) collective-permute-start(bf16[2,512,512]{2,1,0:T(8,128)(2,1)} %collective-permute-done.10), channel_id=1, source_target_pairs={{0,30},{2,0},{4,2},{6,4},{8,6},{10,8},{12,10},{14,12},{16,14},{18,... | collective-permute-start | bytes 3145736 | tf_op jit(solution)/shard_map/ppermute | solution.py:12
  174.5 17.9 %collective-permute-start.20 = (s32[2]{0:T(128)S(1)}, s32[2]{0:T(128)S(1)}, u32[]{:S(2)}, u32[]{:S(2)}) collective-permute-start(s32[2]{0:T(128)S(1)} %collective-permute-done.16), channel_id=1, source_target_pairs={{0,30},{2,0},{4,2},{6,4},{8,6},{10,8},{12,10},{14,12},{16,14},{18,... | collective-permute-start | bytes 32 | tf_op jit(solution)/shard_map/ppermute | solution.py:12
  198.4 22.4 %collective-permute-start.11 = (bf16[1024,384]{1,0:T(8,128)(2,1)}, bf16[1024,384]{1,0:T(8,128)(2,1)}, u32[]{:S(2)}, u32[]{:S(2)}) collective-permute-start(bf16[1024,384]{1,0:T(8,128)(2,1)} %collective-permute-done.7), channel_id=1, source_target_pairs={{0,480},{32,0},{64,32},{96,64},{128,96},{160,128},{192,160},{224,1... | collective-permute-start | bytes 2359304 | tf_op jit(solution)/shard_map/ppermute | solution.py:12
  214.5 30.2 %collective-permute-start.18 = (bf16[2,512,512]{2,1,0:T(8,128)(2,1)}, bf16[2,512,512]{2,1,0:T(8,128)(2,1)}, u32[]{:S(2)}, u32[]{:S(2)}) collective-permute-start(bf16[2,512,512]{2,1,0:T(8,128)(2,1)} %collective-permute-done.14), channel_id=1, source_target_pairs={{0,30},{2,0},{4,2},{6,4},{8,6},{10,8},{12,10},{14,12},{16,14},{18,... | collective-permute-start | bytes 3145736 | tf_op jit(solution)/shard_map/ppermute | solution.py:12
  220.8 21.6 %collective-permute-start.15 = (bf16[1024,384]{1,0:T(8,128)(2,1)}, bf16[1024,384]{1,0:T(8,128)(2,1)}, u32[]{:S(2)}, u32[]{:S(2)}) collective-permute-start(bf16[1024,384]{1,0:T(8,128)(2,1)} %collective-permute-done.11), channel_id=1, source_target_pairs={{0,480},{32,0},{64,32},{96,64},{128,96},{160,128},{192,160},{224,1... | collective-permute-start | bytes 2359304 | tf_op jit(solution)/shard_map/ppermute | solution.py:12
  242.5 18.4 %collective-permute-start.19 = (bf16[1024,384]{1,0:T(8,128)(2,1)}, bf16[1024,384]{1,0:T(8,128)(2,1)}, u32[]{:S(2)}, u32[]{:S(2)}) collective-permute-start(bf16[1024,384]{1,0:T(8,128)(2,1)} %collective-permute-done.15), channel_id=1, source_target_pairs={{0,480},{32,0},{64,32},{96,64},{128,96},{160,128},{192,160},{224,1... | collective-permute-start | bytes 2359304 | tf_op jit(solution)/shard_map/ppermute | solution.py:12
  244.7 23.3 %collective-permute-start.22 = (bf16[2,512,512]{2,1,0:T(8,128)(2,1)}, bf16[2,512,512]{2,1,0:T(8,128)(2,1)}, u32[]{:S(2)}, u32[]{:S(2)}) collective-permute-start(bf16[2,512,512]{2,1,0:T(8,128)(2,1)} %collective-permute-done.18), channel_id=1, source_target_pairs={{0,30},{2,0},{4,2},{6,4},{8,6},{10,8},{12,10},{14,12},{16,14},{18,... | collective-permute-start | bytes 3145736 | tf_op jit(solution)/shard_map/ppermute | solution.py:12
  260.9 17.9 %collective-permute-start.23 = (bf16[1024,384]{1,0:T(8,128)(2,1)}, bf16[1024,384]{1,0:T(8,128)(2,1)S(1)}, u32[]{:S(2)}, u32[]{:S(2)}) collective-permute-start(bf16[1024,384]{1,0:T(8,128)(2,1)} %collective-permute-done.19), channel_id=1, source_target_pairs={{0,480},{32,0},{64,32},{96,64},{128,96},{160,128},{192,160},{224,1... | collective-permute-start | bytes 2359304 | tf_op jit(solution)/shard_map/ppermute | solution.py:12
  268.0 23.6 %collective-permute-start.26 = (bf16[2,512,512]{2,1,0:T(8,128)(2,1)}, bf16[2,512,512]{2,1,0:T(8,128)(2,1)S(1)}, u32[]{:S(2)}, u32[]{:S(2)}) collective-permute-start(bf16[2,512,512]{2,1,0:T(8,128)(2,1)} %collective-permute-done.22), channel_id=1, source_target_pairs={{0,30},{2,0},{4,2},{6,4},{8,6},{10,8},{12,10},{14,12},{16,14},{18,... | collective-permute-start | bytes 3145736 | tf_op jit(solution)/shard_map/ppermute | solution.py:12
  278.8 21.8 %collective-permute-start.27 = (bf16[1024,384]{1,0:T(8,128)(2,1)S(1)}, bf16[1024,384]{1,0:T(8,128)(2,1)S(1)}, u32[]{:S(2)}, u32[]{:S(2)}) collective-permute-start(bf16[1024,384]{1,0:T(8,128)(2,1)S(1)} %collective-permute-done.23), channel_id=1, source_target_pairs={{0,480},{32,0},{64,32},{96,64},{128,96},{160,128},{192,160},{224,1... | collective-permute-start | bytes 2359304 | tf_op jit(solution)/shard_map/ppermute | solution.py:12
  291.7 22.8 %collective-permute-start.30 = (bf16[2,512,512]{2,1,0:T(8,128)(2,1)S(1)}, bf16[2,512,512]{2,1,0:T(8,128)(2,1)S(1)}, u32[]{:S(2)}, u32[]{:S(2)}) collective-permute-start(bf16[2,512,512]{2,1,0:T(8,128)(2,1)S(1)} %collective-permute-done.26), channel_id=1, source_target_pairs={{0,30},{2,0},{4,2},{6,4},{8,6},{10,8},{12,10},{14,12},{16,14},{18,... | collective-permute-start | bytes 3145736 | tf_op jit(solution)/shard_map/ppermute | solution.py:12
  (9 other events, 95.7 us)
Sparse Core Ops, SparseCore 0:
  323.6 26.4 reduce-scatter.1
where the time goes:
time: 412 us; the launch traced here: 410 us
  starting transfers between devices  142 us (34%)
  waiting for transfers between devices  108 us (26%)
  between operations  64.9 us (16%)
  blocking collectives  49.6 us (12%)
  matrix products  25.2 us (6%)
  other arithmetic  12.9 us (3%)
  local copies, waits for them, and re-layouts  6.23 us (2%)
    ppermute x32, starting transfers between devices, from_behind(): return lax.ppermute(value, axis, pairs)  142 us
    ppermute x32, waiting for transfers between devices, from_behind(): return lax.ppermute(value, axis, pairs)  81.8 us
    psum x1, blocking collectives, local(): column_mass = lax.psum(jnp.sum(inflated, axis=0), ('row', 'layer'))  49.6 us
    reduce_scatter x1, waiting for transfers between devices, local(): lax.psum_scatter(partial_block, 'layer', scatter_dimension=0, tiled=True)  26.6 us
    dot_general x16, matrix products, tile_products(): jnp.dot(tile_data[slot_index], source, preferred_element_type=jnp.float32)  25.2 us
  transfers between devices with their start and end apart: 33, of which 13 were waited for; matrix products, arithmetic and copies ran while one was open for 8% of the time, Pallas kernels for 0%

commit v1 on v0

--- a/solution.py
+++ b/solution.py
@@ -56,7 +56,7 @@
     matrix_order = grid_size * SPAN * tile_size
     shared = lax.psum_scatter(partial_block, "layer", scatter_dimension=0, tiled=True)
     inflated = shared * shared
-    column_mass = lax.psum(jnp.sum(inflated, axis=0), ("row", "layer"))
+    column_mass = lax.psum(lax.psum(jnp.sum(inflated, axis=0), "row"), "layer")
     return inflated / (column_mass / matrix_order + 1e-06)
 
 

time: 412 us -> 397 us (0.964)
  the two profiles are of different devices: /device:TPU:2 before, /device:TPU:1 now
where the time goes in v1:
time: 397 us; the launch traced here: 395 us
  starting transfers between devices  147 us (37%)
  waiting for transfers between devices  106 us (27%)
  between operations  64.7 us (16%)
  blocking collectives  32.9 us (8%)
  matrix products  25.2 us (6%)
  other arithmetic  13.2 us (3%)
  local copies, waits for them, and re-layouts  6.16 us (2%)
    ppermute x32, starting transfers between devices, from_behind(): return lax.ppermute(value, axis, pairs)  147 us
    ppermute x32, waiting for transfers between devices, from_behind(): return lax.ppermute(value, axis, pairs)  72.4 us
    reduce_scatter x1, waiting for transfers between devices, local(): lax.psum_scatter(partial_block, 'layer', scatter_dimension=0, tiled=True)  33.2 us
    psum x2, blocking collectives, local(): column_mass = lax.psum(lax.psum(jnp.sum(inflated, axis=0), 'row'), 'layer')  32.9 us
    dot_general x16, matrix products, tile_products(): jnp.dot(tile_data[slot_index], source, preferred_element_type=jnp.float32)  25.2 us
  transfers between devices with their start and end apart: 33, of which 12 were waited for; matrix products, arithmetic and copies ran while one was open for 8% of the time, Pallas kernels for 0%

profile of v1, /device:TPU:1, one launch (start us, length us, event | category | flops | bytes accessed | tf_op | source)
XLA Modules:
  0.0 394.7 jit_solution(12059202971121806141)
XLA Ops:
  6.5 5.5 %collective-permute-start = (s32[2]{0:T(128)}, s32[2]{0:T(128)S(1)}, u32[]{:S(2)}, u32[]{:S(2)}) collective-permute-start(s32[2]{0:T(128)} %bitcast.294), channel_id=1, source_target_pairs={{0,16},{2,18},{4,20},{6,22},{8,24},{10,26},{12,28},{14,30},{16,0},... | collective-permute-start | bytes 32 | tf_op jit(solution)/shard_map/ppermute | solution.py:12
  13.9 15.7 %collective-permute-start.3 = (bf16[1024,384]{1,0:T(8,128)(2,1)}, bf16[1024,384]{1,0:T(8,128)(2,1)}, u32[]{:S(2)}, u32[]{:S(2)}) collective-permute-start(bf16[1024,384]{1,0:T(8,128)(2,1)} %bitcast.271), channel_id=1, source_target_pairs={{0,256},{32,288},{64,320},{96,352},{128,384},{160,416},{192,448},{... | collective-permute-start | bytes 2359304 | tf_op jit(solution)/shard_map/ppermute | solution.py:12
  29.6 4.7 %collective-permute-start.2 = (bf16[2,512,512]{2,1,0:T(8,128)(2,1)}, bf16[2,512,512]{2,1,0:T(8,128)(2,1)S(1)}, u32[]{:S(2)}, u32[]{:S(2)}) collective-permute-start(bf16[2,512,512]{2,1,0:T(8,128)(2,1)} %bitcast.270), channel_id=1, source_target_pairs={{0,16},{2,18},{4,20},{6,22},{8,24},{10,26},{12,28},{14,30},{16,0},... | collective-permute-start | bytes 3145736 | tf_op jit(solution)/shard_map/ppermute | solution.py:12
  35.6 5.9 %collective-permute-start.5 = (s32[]{:T(128)}, s32[]{:T(128)}, u32[]{:S(2)}, u32[]{:S(2)}) collective-permute-start(s32[]{:T(128)} %select_n.195), channel_id=1, source_target_pairs={{0,30},{2,0},{4,2},{6,4},{8,6},{10,8},{12,10},{14,12},{16,14},{18,... | collective-permute-start | bytes 20 | tf_op jit(solution)/shard_map/ppermute | solution.py:12
  57.7 5.4 %collective-permute-start.13 = (s32[]{:T(128)}, s32[]{:T(128)}, u32[]{:S(2)}, u32[]{:S(2)}) collective-permute-start(s32[]{:T(128)} %collective-permute-done.9), channel_id=1, source_target_pairs={{0,30},{2,0},{4,2},{6,4},{8,6},{10,8},{12,10},{14,12},{16,14},{18,... | collective-permute-start | bytes 20 | tf_op jit(solution)/shard_map/ppermute | solution.py:12
  70.6 14.0 %collective-permute-start.8 = (s32[2]{0:T(128)S(1)}, s32[2]{0:T(128)S(1)}, u32[]{:S(2)}, u32[]{:S(2)}) collective-permute-start(s32[2]{0:T(128)S(1)} %collective-permute-done.4), channel_id=1, source_target_pairs={{0,30},{2,0},{4,2},{6,4},{8,6},{10,8},{12,10},{14,12},{16,14},{18,... | collective-permute-start | bytes 32 | tf_op jit(solution)/shard_map/ppermute | solution.py:12
  90.2 6.9 %collective-permute-start.21 = (s32[]{:T(128)}, s32[]{:T(128)}, u32[]{:S(2)}, u32[]{:S(2)}) collective-permute-start(s32[]{:T(128)} %collective-permute-done.17), channel_id=1, source_target_pairs={{0,30},{2,0},{4,2},{6,4},{8,6},{10,8},{12,10},{14,12},{16,14},{18,... | collective-permute-start | bytes 20 | tf_op jit(solution)/shard_map/ppermute | solution.py:12
  111.6 13.5 %collective-permute-done.25 = s32[]{:T(128)} collective-permute-done((s32[]{:T(128)}, s32[]{:T(128)}, u32[]{:S(2)}, u32[]{:S(2)}) %collective-permute-start.25) | collective-permute-done | bytes 36 | tf_op jit(solution)/shard_map/ppermute | solution.py:12
  126.2 5.5 %collective-permute-start.29 = (s32[]{:T(128)}, s32[]{:T(128)}, u32[]{:S(2)}, u32[]{:S(2)}) collective-permute-start(s32[]{:T(128)} %collective-permute-done.25), channel_id=1, source_target_pairs={{0,30},{2,0},{4,2},{6,4},{8,6},{10,8},{12,10},{14,12},{16,14},{18,... | collective-permute-start | bytes 20 | tf_op jit(solution)/shard_map/ppermute | solution.py:12
  143.2 14.7 %collective-permute-done.16 = s32[2]{0:T(128)S(1)} collective-permute-done((s32[2]{0:T(128)S(1)}, s32[2]{0:T(128)S(1)}, u32[]{:S(2)}, u32[]{:S(2)}) %collective-permute-start.16) | collective-permute-done | bytes 40 | tf_op jit(solution)/shard_map/ppermute | solution.py:12
  164.8 4.4 %collective-permute-start.7 = (bf16[1024,384]{1,0:T(8,128)(2,1)S(1)}, bf16[1024,384]{1,0:T(8,128)(2,1)}, u32[]{:S(2)}, u32[]{:S(2)}) collective-permute-start(bf16[1024,384]{1,0:T(8,128)(2,1)S(1)} %broadcast_select_fusion.1), channel_id=1, source_target_pairs={{0,480},{32,0},{64,32},{96,64},{128,96},{160,128},{192,160},{224,1... | collective-permute-start | bytes 2359304 | tf_op jit(solution)/shard_map/ppermute | solution.py:12
  169.3 5.5 %collective-permute-start.14 = (bf16[2,512,512]{2,1,0:T(8,128)(2,1)}, bf16[2,512,512]{2,1,0:T(8,128)(2,1)}, u32[]{:S(2)}, u32[]{:S(2)}) collective-permute-start(bf16[2,512,512]{2,1,0:T(8,128)(2,1)} %collective-permute-done.10), channel_id=1, source_target_pairs={{0,30},{2,0},{4,2},{6,4},{8,6},{10,8},{12,10},{14,12},{16,14},{18,... | collective-permute-start | bytes 3145736 | tf_op jit(solution)/shard_map/ppermute | solution.py:12
  176.8 14.2 %collective-permute-done.20 = s32[2]{0:T(128)S(1)} collective-permute-done((s32[2]{0:T(128)S(1)}, s32[2]{0:T(128)S(1)}, u32[]{:S(2)}, u32[]{:S(2)}) %collective-permute-start.20) | collective-permute-done | bytes 40 | tf_op jit(solution)/shard_map/ppermute | solution.py:12
  199.0 7.4 %collective-permute-start.24 = (s32[2]{0:T(128)S(1)}, s32[2]{0:T(128)S(1)}, u32[]{:S(2)}, u32[]{:S(2)}) collective-permute-start(s32[2]{0:T(128)S(1)} %collective-permute-done.20), channel_id=1, source_target_pairs={{0,30},{2,0},{4,2},{6,4},{8,6},{10,8},{12,10},{14,12},{16,14},{18,... | collective-permute-start | bytes 32 | tf_op jit(solution)/shard_map/ppermute | solution.py:12
  212.9 6.9 %collective-permute-start.18 = (bf16[2,512,512]{2,1,0:T(8,128)(2,1)}, bf16[2,512,512]{2,1,0:T(8,128)(2,1)}, u32[]{:S(2)}, u32[]{:S(2)}) collective-permute-start(bf16[2,512,512]{2,1,0:T(8,128)(2,1)} %collective-permute-done.14), channel_id=1, source_target_pairs={{0,30},{2,0},{4,2},{6,4},{8,6},{10,8},{12,10},{14,12},{16,14},{18,... | collective-permute-start | bytes 3145736 | tf_op jit(solution)/shard_map/ppermute | solution.py:12
  223.8 10.1 %collective-permute-done.28 = s32[2]{0:T(128)S(1)} collective-permute-done((s32[2]{0:T(128)S(1)}, s32[2]{0:T(128)S(1)}, u32[]{:S(2)}, u32[]{:S(2)}) %collective-permute-start.28) | collective-permute-done | bytes 40 | tf_op jit(solution)/shard_map/ppermute | solution.py:12
  241.7 7.4 %collective-permute-start.22 = (bf16[2,512,512]{2,1,0:T(8,128)(2,1)}, bf16[2,512,512]{2,1,0:T(8,128)(2,1)}, u32[]{:S(2)}, u32[]{:S(2)}) collective-permute-start(bf16[2,512,512]{2,1,0:T(8,128)(2,1)} %collective-permute-done.18), channel_id=1, source_target_pairs={{0,30},{2,0},{4,2},{6,4},{8,6},{10,8},{12,10},{14,12},{16,14},{18,... | collective-permute-start | bytes 3145736 | tf_op jit(solution)/shard_map/ppermute | solution.py:12
  262.3 7.4 %collective-permute-start.26 = (bf16[2,512,512]{2,1,0:T(8,128)(2,1)}, bf16[2,512,512]{2,1,0:T(8,128)(2,1)S(1)}, u32[]{:S(2)}, u32[]{:S(2)}) collective-permute-start(bf16[2,512,512]{2,1,0:T(8,128)(2,1)} %collective-permute-done.22), channel_id=1, source_target_pairs={{0,30},{2,0},{4,2},{6,4},{8,6},{10,8},{12,10},{14,12},{16,14},{18,... | collective-permute-start | bytes 3145736 | tf_op jit(solution)/shard_map/ppermute | solution.py:12
  283.9 7.3 %collective-permute-start.30 = (bf16[2,512,512]{2,1,0:T(8,128)(2,1)S(1)}, bf16[2,512,512]{2,1,0:T(8,128)(2,1)S(1)}, u32[]{:S(2)}, u32[]{:S(2)}) collective-permute-start(bf16[2,512,512]{2,1,0:T(8,128)(2,1)S(1)} %collective-permute-done.26), channel_id=1, source_target_pairs={{0,30},{2,0},{4,2},{6,4},{8,6},{10,8},{12,10},{14,12},{16,14},{18,... | collective-permute-start | bytes 3145736 | tf_op jit(solution)/shard_map/ppermute | solution.py:12
  303.3 6.1 %collective-permute-done.31 = bf16[1024,384]{1,0:T(8,128)(2,1)S(1)} collective-permute-done((bf16[1024,384]{1,0:T(8,128)(2,1)S(1)}, bf16[1024,384]{1,0:T(8,128)(2,1)S(1)}, u32[]{:S(2)}, u32[]{:S(2)}) %collective-permute-start.31) | collective-permute-done | bytes 786464 | tf_op jit(solution)/shard_map/ppermute | solution.py:12
  312.1 6.3 %fusion = f32[1024,384]{1,0:T(8,128)} fusion(f32[512,384]{1,0:T(8,128)} %fusion.15, f32[1024]{0:T(1024)S(1)} %bitcast.292, f32[512,384]{1,0:T(8,128)} %fusion.16, f32[1024]{0:T(1024)S(1)} %bitcast.293, f32[512,384]{1,0:T(8,128)} %fusion.17, f32[1024]{0:T(1024)S(1)} %bitcast.290, f32[512,384]{1,0:T(8,128)} %fusion.18, f32[1024]{0:T(1024)S(1)} %bitcast.291, ...), kind=kLoop, calls=%fused_computation.1 | loop fusion | flops 12189696 | bytes 14221312 | tf_op jit(solution)/shard_map/add | solution.py:26
  318.4 33.2 %reduce-scatter.2.cloned.1.call-done = f32[512,384]{1,0:T(8,128)} async-done(((f32[1024,384]{1,0:T(8,128)}), f32[512,384]{1,0:T(8,128)}) %reduce-scatter.2.cloned.1.call-update) | async-done | bytes 786448 | tf_op jit(solution)/shard_map/reduce_scatter | solution.py:57
  352.8 24.0 %psum.14 = f32[384]{0:T(512)S(1)} all-reduce(f32[384]{0:T(512)S(1)} %multiply_reduce_fusion), channel_id=1, replica_groups=mesh['row'=16,'col'=16,'layer'=2] {'row'}, use_global_device_ids=true, to_apply=%region_2.3 | all-reduce | flops 384 | bytes 3072 | tf_op jit(solution)/shard_map/psum | solution.py:59
  376.8 8.9 %psum.15 = f32[384]{0:T(512)S(1)} all-reduce(f32[384]{0:T(512)S(1)} %psum.14), channel_id=1, replica_groups=mesh['row'=16,'col'=16,'layer'=2] {'layer'}, use_global_device_ids=true, to_apply=%region_3.4 | all-reduce | flops 384 | bytes 3072 | tf_op jit(solution)/shard_map/psum | solution.py:59
  (124 shorter events, 88.9 us)
Async XLA Ops:
  6.5 345.0 %reduce-scatter.2.cloned.1.call-start = ((), (), s32[]{:S(2)}) async-start(), calls=%async_computation.1 | async-start | bytes 2359296 | tf_op jit(solution)/shard_map/reduce_scatter | solution.py:57
  6.5 35.0 %collective-permute-start = (s32[2]{0:T(128)}, s32[2]{0:T(128)S(1)}, u32[]{:S(2)}, u32[]{:S(2)}) collective-permute-start(s32[2]{0:T(128)} %bitcast.294), channel_id=1, source_target_pairs={{0,16},{2,18},{4,20},{6,22},{8,24},{10,26},{12,28},{14,30},{16,0},... | collective-permute-start | bytes 32 | tf_op jit(solution)/shard_map/ppermute | solution.py:12
  12.0 22.9 %collective-permute-start.1 = (s32[]{:T(128)}, s32[]{:T(128)}, u32[]{:S(2)}, u32[]{:S(2)}) collective-permute-start(s32[]{:T(128)} %bitcast.2), channel_id=1, source_target_pairs={{0,16},{2,18},{4,20},{6,22},{8,24},{10,26},{12,28},{14,30},{16,0},... | collective-permute-start | bytes 20 | tf_op jit(solution)/shard_map/ppermute | solution.py:12
  13.9 149.4 %collective-permute-start.3 = (bf16[1024,384]{1,0:T(8,128)(2,1)}, bf16[1024,384]{1,0:T(8,128)(2,1)}, u32[]{:S(2)}, u32[]{:S(2)}) collective-permute-start(bf16[1024,384]{1,0:T(8,128)(2,1)} %bitcast.271), channel_id=1, source_target_pairs={{0,256},{32,288},{64,320},{96,352},{128,384},{160,416},{192,448},{... | collective-permute-start | bytes 2359304 | tf_op jit(solution)/shard_map/ppermute | solution.py:12
  29.6 73.3 %collective-permute-start.2 = (bf16[2,512,512]{2,1,0:T(8,128)(2,1)}, bf16[2,512,512]{2,1,0:T(8,128)(2,1)S(1)}, u32[]{:S(2)}, u32[]{:S(2)}) collective-permute-start(bf16[2,512,512]{2,1,0:T(8,128)(2,1)} %bitcast.270), channel_id=1, source_target_pairs={{0,16},{2,18},{4,20},{6,22},{8,24},{10,26},{12,28},{14,30},{16,0},... | collective-permute-start | bytes 3145736 | tf_op jit(solution)/shard_map/ppermute | solution.py:12
  47.7 15.5 %collective-permute-start.4 = (s32[2]{0:T(128)S(1)}, s32[2]{0:T(128)S(1)}, u32[]{:S(2)}, u32[]{:S(2)}) collective-permute-start(s32[2]{0:T(128)S(1)} %broadcast_select_fusion.2), channel_id=1, source_target_pairs={{0,30},{2,0},{4,2},{6,4},{8,6},{10,8},{12,10},{14,12},{16,14},{18,... | collective-permute-start | bytes 32 | tf_op jit(solution)/shard_map/ppermute | solution.py:12
  70.6 26.5 %collective-permute-start.8 = (s32[2]{0:T(128)S(1)}, s32[2]{0:T(128)S(1)}, u32[]{:S(2)}, u32[]{:S(2)}) collective-permute-start(s32[2]{0:T(128)S(1)} %collective-permute-done.4), channel_id=1, source_target_pairs={{0,30},{2,0},{4,2},{6,4},{8,6},{10,8},{12,10},{14,12},{16,14},{18,... | collective-permute-start | bytes 32 | tf_op jit(solution)/shard_map/ppermute | solution.py:12
  90.2 18.1 %collective-permute-start.21 = (s32[]{:T(128)}, s32[]{:T(128)}, u32[]{:S(2)}, u32[]{:S(2)}) collective-permute-start(s32[]{:T(128)} %collective-permute-done.17), channel_id=1, source_target_pairs={{0,30},{2,0},{4,2},{6,4},{8,6},{10,8},{12,10},{14,12},{16,14},{18,... | collective-permute-start | bytes 20 | tf_op jit(solution)/shard_map/ppermute | solution.py:12
  104.3 33.7 %collective-permute-start.6 = (bf16[2,512,512]{2,1,0:T(8,128)(2,1)S(1)}, bf16[2,512,512]{2,1,0:T(8,128)(2,1)S(1)}, u32[]{:S(2)}, u32[]{:S(2)}) collective-permute-start(bf16[2,512,512]{2,1,0:T(8,128)(2,1)S(1)} %broadcast_select_fusion), channel_id=1, source_target_pairs={{0,30},{2,0},{4,2},{6,4},{8,6},{10,8},{12,10},{14,12},{16,14},{18,... | collective-permute-start | bytes 3145736 | tf_op jit(solution)/shard_map/ppermute | solution.py:12
  106.4 25.4 %collective-permute-start.12 = (s32[2]{0:T(128)S(1)}, s32[2]{0:T(128)S(1)}, u32[]{:S(2)}, u32[]{:S(2)}) collective-permute-start(s32[2]{0:T(128)S(1)} %collective-permute-done.8), channel_id=1, source_target_pairs={{0,30},{2,0},{4,2},{6,4},{8,6},{10,8},{12,10},{14,12},{16,14},{18,... | collective-permute-start | bytes 32 | tf_op jit(solution)/shard_map/ppermute | solution.py:12
  137.9 31.3 %collective-permute-start.10 = (bf16[2,512,512]{2,1,0:T(8,128)(2,1)S(1)}, bf16[2,512,512]{2,1,0:T(8,128)(2,1)}, u32[]{:S(2)}, u32[]{:S(2)}) collective-permute-start(bf16[2,512,512]{2,1,0:T(8,128)(2,1)S(1)} %collective-permute-done.6), channel_id=1, source_target_pairs={{0,30},{2,0},{4,2},{6,4},{8,6},{10,8},{12,10},{14,12},{16,14},{18,... | collective-permute-start | bytes 3145736 | tf_op jit(solution)/shard_map/ppermute | solution.py:12
  141.2 16.6 %collective-permute-start.16 = (s32[2]{0:T(128)S(1)}, s32[2]{0:T(128)S(1)}, u32[]{:S(2)}, u32[]{:S(2)}) collective-permute-start(s32[2]{0:T(128)S(1)} %collective-permute-done.12), channel_id=1, source_target_pairs={{0,30},{2,0},{4,2},{6,4},{8,6},{10,8},{12,10},{14,12},{16,14},{18,... | collective-permute-start | bytes 32 | tf_op jit(solution)/shard_map/ppermute | solution.py:12
  164.8 32.0 %collective-permute-start.7 = (bf16[1024,384]{1,0:T(8,128)(2,1)S(1)}, bf16[1024,384]{1,0:T(8,128)(2,1)}, u32[]{:S(2)}, u32[]{:S(2)}) collective-permute-start(bf16[1024,384]{1,0:T(8,128)(2,1)S(1)} %broadcast_select_fusion.1), channel_id=1, source_target_pairs={{0,480},{32,0},{64,32},{96,64},{128,96},{160,128},{192,160},{224,1... | collective-permute-start | bytes 2359304 | tf_op jit(solution)/shard_map/ppermute | solution.py:12
  169.3 43.6 %collective-permute-start.14 = (bf16[2,512,512]{2,1,0:T(8,128)(2,1)}, bf16[2,512,512]{2,1,0:T(8,128)(2,1)}, u32[]{:S(2)}, u32[]{:S(2)}) collective-permute-start(bf16[2,512,512]{2,1,0:T(8,128)(2,1)} %collective-permute-done.10), channel_id=1, source_target_pairs={{0,30},{2,0},{4,2},{6,4},{8,6},{10,8},{12,10},{14,12},{16,14},{18,... | collective-permute-start | bytes 3145736 | tf_op jit(solution)/shard_map/ppermute | solution.py:12
  174.9 16.2 %collective-permute-start.20 = (s32[2]{0:T(128)S(1)}, s32[2]{0:T(128)S(1)}, u32[]{:S(2)}, u32[]{:S(2)}) collective-permute-start(s32[2]{0:T(128)S(1)} %collective-permute-done.16), channel_id=1, source_target_pairs={{0,30},{2,0},{4,2},{6,4},{8,6},{10,8},{12,10},{14,12},{16,14},{18,... | collective-permute-start | bytes 32 | tf_op jit(solution)/shard_map/ppermute | solution.py:12
  196.8 23.1 %collective-permute-start.11 = (bf16[1024,384]{1,0:T(8,128)(2,1)}, bf16[1024,384]{1,0:T(8,128)(2,1)}, u32[]{:S(2)}, u32[]{:S(2)}) collective-permute-start(bf16[1024,384]{1,0:T(8,128)(2,1)} %collective-permute-done.7), channel_id=1, source_target_pairs={{0,480},{32,0},{64,32},{96,64},{128,96},{160,128},{192,160},{224,1... | collective-permute-start | bytes 2359304 | tf_op jit(solution)/shard_map/ppermute | solution.py:12
  212.9 28.8 %collective-permute-start.18 = (bf16[2,512,512]{2,1,0:T(8,128)(2,1)}, bf16[2,512,512]{2,1,0:T(8,128)(2,1)}, u32[]{:S(2)}, u32[]{:S(2)}) collective-permute-start(bf16[2,512,512]{2,1,0:T(8,128)(2,1)} %collective-permute-done.14), channel_id=1, source_target_pairs={{0,30},{2,0},{4,2},{6,4},{8,6},{10,8},{12,10},{14,12},{16,14},{18,... | collective-permute-start | bytes 3145736 | tf_op jit(solution)/shard_map/ppermute | solution.py:12
  219.9 19.7 %collective-permute-start.15 = (bf16[1024,384]{1,0:T(8,128)(2,1)}, bf16[1024,384]{1,0:T(8,128)(2,1)}, u32[]{:S(2)}, u32[]{:S(2)}) collective-permute-start(bf16[1024,384]{1,0:T(8,128)(2,1)} %collective-permute-done.11), channel_id=1, source_target_pairs={{0,480},{32,0},{64,32},{96,64},{128,96},{160,128},{192,160},{224,1... | collective-permute-start | bytes 2359304 | tf_op jit(solution)/shard_map/ppermute | solution.py:12
  241.7 20.6 %collective-permute-start.22 = (bf16[2,512,512]{2,1,0:T(8,128)(2,1)}, bf16[2,512,512]{2,1,0:T(8,128)(2,1)}, u32[]{:S(2)}, u32[]{:S(2)}) collective-permute-start(bf16[2,512,512]{2,1,0:T(8,128)(2,1)} %collective-permute-done.18), channel_id=1, source_target_pairs={{0,30},{2,0},{4,2},{6,4},{8,6},{10,8},{12,10},{14,12},{16,14},{18,... | collective-permute-start | bytes 3145736 | tf_op jit(solution)/shard_map/ppermute | solution.py:12
  252.6 20.4 %collective-permute-start.23 = (bf16[1024,384]{1,0:T(8,128)(2,1)}, bf16[1024,384]{1,0:T(8,128)(2,1)S(1)}, u32[]{:S(2)}, u32[]{:S(2)}) collective-permute-start(bf16[1024,384]{1,0:T(8,128)(2,1)} %collective-permute-done.19), channel_id=1, source_target_pairs={{0,480},{32,0},{64,32},{96,64},{128,96},{160,128},{192,160},{224,1... | collective-permute-start | bytes 2359304 | tf_op jit(solution)/shard_map/ppermute | solution.py:12
  262.3 21.6 %collective-permute-start.26 = (bf16[2,512,512]{2,1,0:T(8,128)(2,1)}, bf16[2,512,512]{2,1,0:T(8,128)(2,1)S(1)}, u32[]{:S(2)}, u32[]{:S(2)}) collective-permute-start(bf16[2,512,512]{2,1,0:T(8,128)(2,1)} %collective-permute-done.22), channel_id=1, source_target_pairs={{0,30},{2,0},{4,2},{6,4},{8,6},{10,8},{12,10},{14,12},{16,14},{18,... | collective-permute-start | bytes 3145736 | tf_op jit(solution)/shard_map/ppermute | solution.py:12
  272.9 20.8 %collective-permute-start.27 = (bf16[1024,384]{1,0:T(8,128)(2,1)S(1)}, bf16[1024,384]{1,0:T(8,128)(2,1)S(1)}, u32[]{:S(2)}, u32[]{:S(2)}) collective-permute-start(bf16[1024,384]{1,0:T(8,128)(2,1)S(1)} %collective-permute-done.23), channel_id=1, source_target_pairs={{0,480},{32,0},{64,32},{96,64},{128,96},{160,128},{192,160},{224,1... | collective-permute-start | bytes 2359304 | tf_op jit(solution)/shard_map/ppermute | solution.py:12
  283.9 25.5 %collective-permute-start.30 = (bf16[2,512,512]{2,1,0:T(8,128)(2,1)S(1)}, bf16[2,512,512]{2,1,0:T(8,128)(2,1)S(1)}, u32[]{:S(2)}, u32[]{:S(2)}) collective-permute-start(bf16[2,512,512]{2,1,0:T(8,128)(2,1)S(1)} %collective-permute-done.26), channel_id=1, source_target_pairs={{0,30},{2,0},{4,2},{6,4},{8,6},{10,8},{12,10},{14,12},{16,14},{18,... | collective-permute-start | bytes 3145736 | tf_op jit(solution)/shard_map/ppermute | solution.py:12
  293.8 15.6 %collective-permute-start.31 = (bf16[1024,384]{1,0:T(8,128)(2,1)S(1)}, bf16[1024,384]{1,0:T(8,128)(2,1)S(1)}, u32[]{:S(2)}, u32[]{:S(2)}) collective-permute-start(bf16[1024,384]{1,0:T(8,128)(2,1)S(1)} %collective-permute-done.27), channel_id=1, source_target_pairs={{0,480},{32,0},{64,32},{96,64},{128,96},{160,128},{192,160},{224,1... | collective-permute-start | bytes 2359304 | tf_op jit(solution)/shard_map/ppermute | solution.py:12
  (9 other events, 97.8 us)
Sparse Core Ops, SparseCore 0:
  318.5 32.9 reduce-scatter.1
